TPU v7x, 512 devices: a whole 4x4x16 slice. The times are simulated.
512 devices in a mesh: row: 32 (over y, z_hi, x), col: 16 (over z_lo, core).
Axes of the slice: x: 4, y: 4, z: 16 (z_hi: 2, z_lo: 8; z = z_hi * 8 + z_lo), core: 2. Of those that a mesh axis runs over, the one named last changes fastest.
Arguments:
- nodes: bfloat16 [2048, 512], P(('row', 'col')), may hold values from -50 to 50
- coords: float32 [3, 2048], P(None, ('row', 'col')), may hold values from -18 to 18
- atom_types: int32 [2048], P(('row', 'col')), may hold values from 0 to 29
- segment_ids: int32 [2048], P(('row', 'col')), may hold values from 0 to 1
- pair_mask: int32 [2048, 2048], P('row', 'col'), may hold values 0 or 1
- pair_bias: bfloat16 [64, 2048, 2048], P(None, 'row', 'col'), may hold values from -10 to 310
- ln_gain: float32 [512], replicated, may hold values from 0.1 to 1.9
- w_qkv: bfloat16 [512, 1536], replicated, may hold values from -0.25 to 0.25
- gauss_mul: float32 [60, 60], replicated, may hold values from 0.25 to 1.75
- gauss_add: float32 [60, 60], replicated, may hold values from -4 to 4
- gauss_mean: float32 [128], replicated, may hold values from 0 to 16
- gauss_width: float32 [128], replicated, may hold values from 0.5 to 2.5
- w_gauss: bfloat16 [128, 128], replicated, may hold values from -2 to 2
- w_heads: bfloat16 [128, 64], replicated, may hold values from -2 to 2
- w_coord1: bfloat16 [64, 64], replicated, may hold values from -0.75 to 0.75
- w_coord2: bfloat16 [64], replicated, may hold values from -0.75 to 0.75
Outputs:
- attended: bfloat16 [2048, 512], P(('row', 'col'))
- moved: float32 [3, 2048], P(None, ('row', 'col'))
All inputs are finite; a program needn't handle non-finite values. No bound on the sum of `pair_mask` on one device may be relied on, other than what follows from the above.
Results may differ from a plain program's by a relative error of at most 0.015.
Values may be sent and summed in bfloat16 or wider, within the bound.
A program may use at most 64 MiB of HBM per device.

v0:
```python
import math
import jax
import jax.numpy as jnp
from jax import lax
from jax.sharding import PartitionSpec as P

ln_epsilon = 1e-05
masked_fill = -1000000000.0
root_shift = 0.01


def combined_all(value, axis, join):
    pieces = jax.tree.map(lambda part: lax.all_gather(part, axis), value)
    head = jax.tree.map(lambda part: part[0], pieces)
    tail = jax.tree.map(lambda part: part[1:], pieces)
    total, _ = lax.scan(lambda total, piece: (join(total, piece), None), head, tail)
    return total


def layer_normed(nodes, ln_gain):
    features = nodes.astype(jnp.float32)
    row_mean = jnp.mean(features, axis=1, keepdims=True)
    centred = features - row_mean
    spread = jnp.mean(centred * centred, axis=1, keepdims=True)
    return (centred * lax.rsqrt(spread + ln_epsilon) * ln_gain[None, :]).astype(jnp.bfloat16)


def gaussians(expanded, gauss_mean, gauss_width):
    scaled = (expanded[None, :, :] - gauss_mean[:, None, None]) / gauss_width[:, None, None]
    norming = math.sqrt(2.0 * math.pi) * gauss_width[:, None, None]
    return (jnp.exp(-0.5 * scaled * scaled) / norming).astype(jnp.bfloat16)


def shards(
    nodes,
    coords,
    atom_types,
    segment_ids,
    pair_mask,
    pair_bias,
    ln_gain,
    w_qkv,
    gauss_mul,
    gauss_add,
    gauss_mean,
    gauss_width,
    w_gauss,
    w_heads,
    w_coord1,
    w_coord2,
):
    col_count = lax.axis_size("col")
    row_count = lax.axis_size("row")
    col_index = lax.axis_index("col")
    row_index = lax.axis_index("row")
    own_rows = nodes.shape[0]
    query_rows = own_rows * col_count
    key_cols = own_rows * row_count
    model_width = nodes.shape[1]
    head_count = pair_bias.shape[0]
    head_dim = model_width // head_count
    kind_count = gauss_mul.shape[0]
    all_atoms = own_rows * row_count * col_count
    highest = lax.Precision.HIGHEST
    normed = layer_normed(nodes, ln_gain)
    kinds = atom_types + kind_count // 2 * segment_ids
    own_table = jnp.concatenate([coords, kinds.astype(jnp.float32)[None, :]], axis=0)
    atom_table = lax.all_gather(own_table, ("row", "col"), axis=1, tiled=True)
    query_table = lax.dynamic_slice_in_dim(atom_table, row_index * query_rows, query_rows, 1)
    key_table = lax.dynamic_slice_in_dim(atom_table, col_index * key_cols, key_cols, 1)
    projected = jnp.dot(
        lax.all_gather(normed, "col", axis=0, tiled=True), w_qkv, preferred_element_type=jnp.float32
    ).astype(jnp.bfloat16)
    queries = projected[:, :model_width].reshape(query_rows, head_count, head_dim)
    row_keys = projected[:, model_width:]
    every_key = lax.all_gather(row_keys, "row", axis=0, tiled=True)
    col_keys = lax.dynamic_slice_in_dim(every_key, col_index * key_cols, key_cols, 0)
    keys_block = col_keys[:, :model_width].reshape(key_cols, head_count, head_dim)
    values_block = col_keys[:, model_width:].reshape(key_cols, head_count, head_dim)
    offsets = query_table[:3, :, None] - key_table[:3, None, :]
    distance = jnp.sqrt(jnp.sum(offsets * offsets, axis=0) + root_shift)
    kind_range = jnp.arange(kind_count, dtype=jnp.float32)
    query_onehot = (query_table[3][:, None] == kind_range[None, :]).astype(jnp.float32)
    key_onehot = (key_table[3][:, None] == kind_range[None, :]).astype(jnp.float32)
    both_tables = jnp.concatenate([gauss_mul, gauss_add], axis=1)
    row_lookup = jnp.dot(query_onehot, both_tables, precision=highest)
    scale_pair = jnp.dot(row_lookup[:, :kind_count], key_onehot.T, precision=highest)
    shift_pair = jnp.dot(row_lookup[:, kind_count:], key_onehot.T, precision=highest)
    expanded = scale_pair * distance + shift_pair
    features = gaussians(expanded, gauss_mean, gauss_width)
    hidden = jax.nn.gelu(
        jnp.einsum("kij,kl->lij", features, w_gauss, preferred_element_type=jnp.float32)
    ).astype(jnp.bfloat16)
    geometry = jnp.einsum("kij,kh->hij", hidden, w_heads, preferred_element_type=jnp.float32)
    affinity = jnp.einsum(
        "ihd,jhd->hij", queries, keys_block, preferred_element_type=jnp.float32
    ) / math.sqrt(head_dim)
    logits = pair_bias.astype(jnp.float32) + geometry + affinity
    pair_new = logits.astype(jnp.bfloat16)
    mixed = jax.nn.gelu(
        jnp.einsum("hij,hg->gij", pair_new, w_coord1, preferred_element_type=jnp.float32)
    ).astype(jnp.bfloat16)
    strength = jnp.einsum("gij,g->ij", mixed, w_coord2, preferred_element_type=jnp.float32)
    strength = jnp.where(pair_mask == 1, strength, 0.0)
    row_total = jnp.sum(strength, axis=1)
    pulled = jnp.dot(strength, key_table[:3].T, precision=highest)
    displace = (query_table[:3].T * row_total[:, None] - pulled) / all_atoms
    masked = jnp.where(pair_mask[None, :, :] == 1, logits, masked_fill)
    local_max = jnp.max(masked, axis=2)

    def join_partial(earlier, later):
        max_early, total_early, sums_early = earlier
        max_late, total_late, sums_late = later
        joined_max = jnp.maximum(max_early, max_late)
        factor_early = jnp.exp(max_early - joined_max)
        factor_late = jnp.exp(max_late - joined_max)
        joined_total = total_early * factor_early + total_late * factor_late
        row_span = sums_early.shape[0]
        joined_sums = (
            sums_early.reshape(row_span, head_count, head_dim) * factor_early.T[:, :, None]
            + sums_late.reshape(row_span, head_count, head_dim) * factor_late.T[:, :, None]
        )
        return (joined_max, joined_total, joined_sums.reshape(row_span, model_width))

    weights = jnp.exp(masked - local_max[:, :, None])
    denominator = jnp.sum(weights, axis=2)
    numerator = jnp.einsum(
        "hij,jhd->ihd",
        weights.astype(jnp.bfloat16),
        values_block,
        preferred_element_type=jnp.float32,
    ).reshape(query_rows, model_width)
    joined_max, joined_total, joined_sums = combined_all(
        (local_max, denominator, numerator), "col", join_partial
    )
    own_sums = lax.dynamic_slice_in_dim(joined_sums, col_index * own_rows, own_rows, 0)
    own_totals = lax.dynamic_slice_in_dim(joined_total, col_index * own_rows, own_rows, 1).T
    own_move = lax.psum_scatter(displace, "col", scatter_dimension=0, tiled=True)
    attended = (
        (own_sums.reshape(own_rows, head_count, head_dim) / own_totals[:, :, None])
        .reshape(own_rows, model_width)
        .astype(jnp.bfloat16)
    )
    moved = coords + own_move.T
    return (attended, moved)


def solution(mesh):
    in_specs = (
        P(("row", "col"), None),
        P(None, ("row", "col")),
        P(("row", "col")),
        P(("row", "col")),
        P("row", "col"),
        P(None, "row", "col"),
        P(),
        P(),
        P(),
        P(),
        P(),
        P(),
        P(),
        P(),
        P(),
        P(),
    )
    out_specs = (P(("row", "col"), None), P(None, ("row", "col")))
    return jax.shard_map(shards, mesh=mesh, in_specs=in_specs, out_specs=out_specs, check_vma=False)
```

profile of v0, /device:TPU:258, one launch (start us, length us, event | category | flops | bytes accessed | tf_op | source)
XLA Modules:
  0.0 1059.6 jit_solution(14597980474348112790)
XLA Ops:
  7.3 0.9 convert_reduce_fusion
  8.2 0.9 fusion.69
  9.8 29.0 %all-gather.3 = bf16[16,4,512]{2,1,0:T(4,128)(2,1)S(1)} all-gather(bf16[1,4,512]{2,1,0:T(4,128)(2,1)S(1)} %fusion.73), channel_id=1, replica_groups=mesh['row'=32,'col'=16] {'col'}, dimensions={0}, use_global_device_ids=true | all-gather | bytes 69632 | tf_op jit(solution)/shard_map/all_gather | solution.py:72
  40.3 860.5 %all-gather.2 = f32[512,4,4]{2,1,0:T(4,128)S(1)} all-gather(f32[1,4,4]{2,1,0:T(4,128)S(1)} %bitcast.132), channel_id=1, replica_groups=mesh['row'=32,'col'=16] {'row','col'}, dimensions={0}, use_global_device_ids=true | all-gather | bytes 32832 | tf_op jit(solution)/shard_map/all_gather | solution.py:68
  902.0 1.0 fusion.89
  903.2 1.8 fusion.48
  905.1 6.5 fusion.25
  911.6 2.7 fusion.38
  914.4 2.3 select_reduce_fusion
  916.7 1.3 fusion.31
  919.7 1.3 dynamic-slice.2
  921.7 28.3 %all-gather.1 = f32[1024,64]{1,0:T(8,128)S(1)} all-gather(f32[64,64]{1,0:T(8,128)S(1)} %copy.113), channel_id=3, replica_groups=mesh['row'=32,'col'=16] {'col'}, dimensions={0}, use_global_device_ids=true | all-gather | bytes 278528 | tf_op jit(solution)/shard_map/all_gather | solution.py:13
  950.1 30.2 %all-gather = f32[1024,64]{1,0:T(8,128)S(1)} all-gather(f32[64,64]{1,0:T(8,128)S(1)} %copy.112), channel_id=2, replica_groups=mesh['row'=32,'col'=16] {'col'}, dimensions={0}, use_global_device_ids=true | all-gather | bytes 278528 | tf_op jit(solution)/shard_map/all_gather | solution.py:13
  980.6 47.1 %all-reduce = f32[64,3]{0,1:T(4,128)S(1)} all-reduce(f32[64,3]{0,1:T(4,128)S(1)} %fusion.39), channel_id=4, replica_groups=mesh['row'=32,'col'=16] {'col'}, use_global_device_ids=true, to_apply=%region_8.9.clone | all-reduce | flops 192 | bytes 1536
  1028.3 0.9 slice_bitcast_fusion
  1029.4 3.0 slice.79
  1032.4 19.2 %while.14 = (s32[]{:T(128)}, f32[64,64]{1,0:T(8,128)S(1)}, f32[64,64]{1,0:T(8,128)S(1)}, f32[64,512]{0,1:T(8,128)S(1)}, f32[15,64,64]{2,1,0:T(8,128)S(1)}, /*ind...) while((s32[]{:T(128)}, f32[64,64]{1,0:T(8,128)S(1)}, f32[64,64]{1,0:T(8,128)S(1)}, ...), condition=%wide.region_6.7_spmd, body=%wide.region_5.6_spmd.sunk | while | flops 126978 | bytes 1163369 | solution.py:16
  1032.5 0.9 constant_dynamic-slice_fusion.5
  1033.8 0.9 constant_dynamic-slice_fusion.5
  1035.0 0.9 constant_dynamic-slice_fusion.5
  1036.3 0.9 constant_dynamic-slice_fusion.5
  1037.6 0.9 constant_dynamic-slice_fusion.5
  1038.9 0.9 constant_dynamic-slice_fusion.5
  1040.2 0.9 constant_dynamic-slice_fusion.5
  1041.5 0.9 constant_dynamic-slice_fusion.5
  1042.7 0.9 constant_dynamic-slice_fusion.5
  1044.0 0.9 constant_dynamic-slice_fusion.5
  1045.3 0.9 constant_dynamic-slice_fusion.5
  1046.6 0.9 constant_dynamic-slice_fusion.5
  1047.9 0.9 constant_dynamic-slice_fusion.5
  1049.2 0.9 constant_dynamic-slice_fusion.5
  1050.5 0.9 constant_dynamic-slice_fusion.5
  (151 shorter events, 12.1 us)
Async XLA Ops:
  7.2 31.7 %copy-start = (bf16[512,1536]{1,0:T(8,128)(2,1)S(1)}, bf16[512,1536]{1,0:T(8,128)(2,1)}, u32[]{:S(2)}) copy-start(bf16[512,1536]{1,0:T(8,128)(2,1)} %param.25) | copy-start | bytes 4718596
  7.2 32.9 %copy-start.10 = (s32[4]{0:T(128)S(1)}, s32[4]{0:T(128)}, u32[]{:S(2)}) copy-start(s32[4]{0:T(128)} %param.21) | copy-start | bytes 52
  7.2 32.9 %copy-start.9 = (s32[4]{0:T(128)S(1)}, s32[4]{0:T(128)}, u32[]{:S(2)}) copy-start(s32[4]{0:T(128)} %param.20) | copy-start | bytes 52
  7.2 32.9 %copy-start.5 = (f32[3,4]{1,0:T(4,128)S(1)}, f32[3,4]{1,0:T(4,128)}, u32[]{:S(2)}) copy-start(f32[3,4]{1,0:T(4,128)} %param.19) | copy-start | bytes 148
  7.2 894.8 %all-gather.7.cloned.1.call-start = ((), (), s32[]{:S(2)}) async-start(), calls=%async_computation | async-start | bytes 4325376 | tf_op jit(solution)/shard_map/all_gather | solution.py:76
  9.8 891.3 %copy-start.11 = (f32[128]{0:T(128)S(1)}, f32[128]{0:T(128)}, u32[]{:S(2)}) copy-start(f32[128]{0:T(128)} %param.29) | copy-start | bytes 1540
  9.8 891.3 %copy-start.2 = (f32[60,60]{1,0:T(8,128)S(1)}, f32[60,60]{1,0:T(8,128)}, u32[]{:S(2)}) copy-start(f32[60,60]{1,0:T(8,128)} %param.27) | copy-start | bytes 43204
  9.8 891.3 %copy-start.3 = (f32[60,60]{1,0:T(8,128)S(1)}, f32[60,60]{1,0:T(8,128)}, u32[]{:S(2)}) copy-start(f32[60,60]{1,0:T(8,128)} %param.26) | copy-start | bytes 43204
  40.0 988.4 %all-gather.9.cloned.1.call-start = ((), (), s32[]{:S(2)}) async-start(), calls=%async_computation.1 | async-start | bytes 2228224 | tf_op jit(solution)/shard_map/all_gather | solution.py:13
  900.8 4.2 copy-start.6
  900.8 4.2 copy-start.7
  900.8 4.2 copy-start.12
  905.1 6.5 copy-start.8
  905.1 6.5 copy-start.13
  911.6 2.7 copy-start.4
  914.3 2.5 copy-start.1
Sparse Core Ops, SparseCore 0:
  40.1 151.4 all-gather.6
  919.8 101.6 all-gather.8
where the time goes:
time: 1060 us
  blocking collectives  995 us (94%)
  local copies, waits for them, and re-layouts  24.8 us (2%)
  between operations  15 us (1%)
  matrix products  13.1 us (1%)
  other arithmetic  10.6 us (1%)
    all_gather x1, blocking collectives, shards(): atom_table = lax.all_gather(own_table, ('row', 'col'), axis=1, tiled=True)  860 us
    all_gather x2, blocking collectives, combined_all(): pieces = jax.tree.map(lambda part: lax.all_gather(part, axis), value)  58.6 us
    unnamed x1, blocking collectives  47.1 us
    all_gather x1, blocking collectives, shards(): lax.all_gather(normed, 'col', axis=0, tiled=True)  29 us
  transfers between devices with their start and end apart: 2, of which 0 were waited for; matrix products, arithmetic and copies ran while one was open for 0% of the time, Pallas kernels for 0%

commit v1 on v0

--- a/solution.py
+++ b/solution.py
@@ -65,7 +65,12 @@
     normed = layer_normed(nodes, ln_gain)
     kinds = atom_types + kind_count // 2 * segment_ids
     own_table = jnp.concatenate([coords, kinds.astype(jnp.float32)[None, :]], axis=0)
-    atom_table = lax.all_gather(own_table, ("row", "col"), axis=1, tiled=True)
+    atom_table = jnp.concatenate(
+        lax.all_to_all(
+            jnp.stack([own_table] * lax.axis_size(("row", "col"))), ("row", "col"), 0, 0
+        ),
+        axis=1,
+    )
     query_table = lax.dynamic_slice_in_dim(atom_table, row_index * query_rows, query_rows, 1)
     key_table = lax.dynamic_slice_in_dim(atom_table, col_index * key_cols, key_cols, 1)
     projected = jnp.dot(

time: 1060 us -> 390 us (0.37)
  the two profiles are of different devices: /device:TPU:258 before, /device:TPU:1 now
where the time goes in v1:
time: 390 us; the launch traced here: 389 us
  blocking collectives  153 us (39%)
  waiting for transfers between devices  152 us (39%)
  local copies, waits for them, and re-layouts  28.7 us (7%)
  starting transfers between devices  15.5 us (4%)
  between operations  15 us (4%)
  matrix products  13.1 us (3%)
  other arithmetic  10.5 us (3%)
    all_gather x1, waiting for transfers between devices, shards(): every_key = lax.all_gather(row_keys, 'row', axis=0, tiled=True)  77.4 us
    all_to_all x1, waiting for transfers between devices, shards(): lax.all_to_all(jnp.stack([own_table] * lax.axis_size(('row', 'col'))), ('...  74.5 us
    all_gather x2, blocking collectives, combined_all(): pieces = jax.tree.map(lambda part: lax.all_gather(part, axis), value)  71.1 us
    unnamed x1, blocking collectives  44.7 us
    all_gather x1, blocking collectives, shards(): lax.all_gather(normed, 'col', axis=0, tiled=True)  37.7 us
    dynamic_slice x30, local copies, waits for them, and re-layouts, combined_all(): lax.scan(lambda total, piece: (join(total, piece), None), head, tail)  15.6 us
    all_to_all x1, starting transfers between devices, shards(): lax.all_to_all(jnp.stack([own_table] * lax.axis_size(('row', 'col'))), ('...  15.5 us
  transfers between devices with their start and end apart: 3, of which 2 were waited for; matrix products, arithmetic and copies ran while one was open for 2% of the time, Pallas kernels for 0%

profile of v1, /device:TPU:1, one launch (start us, length us, event | category | flops | bytes accessed | tf_op | source)
XLA Modules:
  0.0 389.1 jit_solution(3300917331694005998)
XLA Ops:
  9.8 37.7 %all-gather.2 = bf16[16,4,512]{2,1,0:T(4,128)(2,1)S(1)} all-gather(bf16[1,4,512]{2,1,0:T(4,128)(2,1)S(1)} %fusion.73), channel_id=1, replica_groups=mesh['row'=32,'col'=16] {'col'}, dimensions={0}, use_global_device_ids=true | all-gather | bytes 69632 | tf_op jit(solution)/shard_map/all_gather | solution.py:77
  48.7 1.1 stack.2
  49.8 15.5 %all-to-all-start = ((f32[512,4,4]{2,1,0:T(4,128)}), f32[512,4,4]{2,1,0:T(4,128)S(1)}, u32[]{:S(2)}, u32[]{:S(2)}) async-start(f32[512,4,4]{2,1,0:T(4,128)} %stack.2), calls=%async_computation | async-start | bytes 2097152 | tf_op jit(solution)/shard_map/all_to_all | solution.py:69
  65.5 74.5 %all-to-all-done = f32[512,4,4]{2,1,0:T(4,128)S(1)} async-done(((f32[512,4,4]{2,1,0:T(4,128)}), f32[512,4,4]{2,1,0:T(4,128)S(1)}, u32[]{:S(2)}, u32[]{:S(2)}) %all-to-all-start) | async-done | bytes 32800 | tf_op jit(solution)/shard_map/all_to_all | solution.py:69
  140.0 1.0 copy.99
  141.0 1.9 reshape.63
  144.0 77.4 %all-gather.6.cloned.1.call-done = bf16[2048,1024]{1,0:T(8,128)(2,1)} async-done(((bf16[64,1024]{1,0:T(8,128)(2,1)}), bf16[2048,1024]{1,0:T(8,128)(2,1)}) %all-gather.6.cloned.1.call-update) | async-done | bytes 4194320 | tf_op jit(solution)/shard_map/all_gather | solution.py:81
  221.4 1.0 fusion.89
  222.6 1.8 fusion.48
  224.5 6.5 %fusion.25 = f32[64,64,128]{2,0,1:T(8,128)} fusion(f32[64,64,128]{2,1,0:T(8,128)} %fusion.48, f32[128]{0:T(128)S(1)} %broadcast_multiply_fusion.1, f32[128]{0:T(128)S(1)} %copy-done.11, f32[128]{0:T(128)S(1)} %copy-done.12, f32[64,128]{1,0:T(8,128)S(1)} %convolution_add_fusion, bf16[64,64,128]{2,1,0:T(8,128)(2,1)} %param.23, ...), kind=kOutput, calls=%fused_computation.36 | convolution fusion | flops 420478976 | bytes 5326336 | tf_op jit(solution)/shard_map/kij,kh->hij/dot_general | solution.py:99
  231.0 2.7 fusion.38
  233.8 2.3 select_reduce_fusion
  236.2 1.3 fusion.31
  239.1 1.3 dynamic-slice
  241.2 40.3 %all-gather.1 = f32[1024,64]{1,0:T(8,128)S(1)} all-gather(f32[64,64]{1,0:T(8,128)S(1)} %copy.105), channel_id=3, replica_groups=mesh['row'=32,'col'=16] {'col'}, dimensions={0}, use_global_device_ids=true | all-gather | bytes 278528 | tf_op jit(solution)/shard_map/all_gather | solution.py:13
  281.5 30.8 %all-gather = f32[1024,64]{1,0:T(8,128)S(1)} all-gather(f32[64,64]{1,0:T(8,128)S(1)} %copy.104), channel_id=2, replica_groups=mesh['row'=32,'col'=16] {'col'}, dimensions={0}, use_global_device_ids=true | all-gather | bytes 278528 | tf_op jit(solution)/shard_map/all_gather | solution.py:13
  312.5 44.7 %all-reduce = f32[64,3]{0,1:T(4,128)S(1)} all-reduce(f32[64,3]{0,1:T(4,128)S(1)} %fusion.39), channel_id=4, replica_groups=mesh['row'=32,'col'=16] {'col'}, use_global_device_ids=true, to_apply=%region_8.9.clone | all-reduce | flops 192 | bytes 1536
  358.8 3.0 slice.79
  361.9 19.2 %while.14 = (s32[]{:T(128)}, f32[64,64]{1,0:T(8,128)S(1)}, f32[64,64]{1,0:T(8,128)S(1)}, f32[64,512]{0,1:T(8,128)S(1)}, f32[15,64,64]{2,1,0:T(8,128)S(1)}, /*ind...) while((s32[]{:T(128)}, f32[64,64]{1,0:T(8,128)S(1)}, f32[64,64]{1,0:T(8,128)S(1)}, ...), condition=%wide.region_6.7_spmd, body=%wide.region_5.6_spmd.sunk | while | flops 126978 | bytes 1163369 | solution.py:16
  361.9 0.9 constant_dynamic-slice_fusion.5
  363.2 0.9 constant_dynamic-slice_fusion.5
  364.5 0.9 constant_dynamic-slice_fusion.5
  365.8 0.9 constant_dynamic-slice_fusion.5
  367.1 0.9 constant_dynamic-slice_fusion.5
  368.4 0.9 constant_dynamic-slice_fusion.5
  369.6 0.9 constant_dynamic-slice_fusion.5
  370.9 0.9 constant_dynamic-slice_fusion.5
  372.2 0.9 constant_dynamic-slice_fusion.5
  373.5 0.9 constant_dynamic-slice_fusion.5
  374.8 0.9 constant_dynamic-slice_fusion.5
  376.1 0.9 constant_dynamic-slice_fusion.5
  377.4 0.9 constant_dynamic-slice_fusion.5
  (152 shorter events, 16.5 us)
Async XLA Ops:
  7.2 40.4 %copy-start = (bf16[512,1536]{1,0:T(8,128)(2,1)S(1)}, bf16[512,1536]{1,0:T(8,128)(2,1)}, u32[]{:S(2)}) copy-start(bf16[512,1536]{1,0:T(8,128)(2,1)} %param.25) | copy-start | bytes 4718596
  7.2 41.5 %copy-start.10 = (s32[4]{0:T(128)S(1)}, s32[4]{0:T(128)}, u32[]{:S(2)}) copy-start(s32[4]{0:T(128)} %param.21) | copy-start | bytes 52
  7.2 41.5 %copy-start.9 = (s32[4]{0:T(128)S(1)}, s32[4]{0:T(128)}, u32[]{:S(2)}) copy-start(s32[4]{0:T(128)} %param.20) | copy-start | bytes 52
  7.2 41.5 %copy-start.5 = (f32[3,4]{1,0:T(4,128)S(1)}, f32[3,4]{1,0:T(4,128)}, u32[]{:S(2)}) copy-start(f32[3,4]{1,0:T(4,128)} %param.19) | copy-start | bytes 148
  7.2 214.2 %all-gather.6.cloned.1.call-start = ((), (), s32[]{:S(2)}) async-start(), calls=%async_computation.1 | async-start | bytes 4325376 | tf_op jit(solution)/shard_map/all_gather | solution.py:81
  48.0 17.6 %copy-start.11 = (f32[128]{0:T(128)S(1)}, f32[128]{0:T(128)}, u32[]{:S(2)}) copy-start(f32[128]{0:T(128)} %param.29) | copy-start | bytes 1540
  49.8 90.2 %all-to-all-start = ((f32[512,4,4]{2,1,0:T(4,128)}), f32[512,4,4]{2,1,0:T(4,128)S(1)}, u32[]{:S(2)}, u32[]{:S(2)}) async-start(f32[512,4,4]{2,1,0:T(4,128)} %stack.2), calls=%async_computation | async-start | bytes 2097152 | tf_op jit(solution)/shard_map/all_to_all | solution.py:69
  65.3 77.9 %copy-start.2 = (f32[60,60]{1,0:T(8,128)S(1)}, f32[60,60]{1,0:T(8,128)}, u32[]{:S(2)}) copy-start(f32[60,60]{1,0:T(8,128)} %param.27) | copy-start | bytes 43204
  65.3 77.9 %copy-start.3 = (f32[60,60]{1,0:T(8,128)S(1)}, f32[60,60]{1,0:T(8,128)}, u32[]{:S(2)}) copy-start(f32[60,60]{1,0:T(8,128)} %param.26) | copy-start | bytes 43204
  65.3 292.5 %all-gather.8.cloned.1.call-start = ((), (), s32[]{:S(2)}) async-start(), calls=%async_computation.2 | async-start | bytes 2228224 | tf_op jit(solution)/shard_map/all_gather | solution.py:13
  142.9 81.5 %copy-start.6 = (bf16[128,128]{1,0:T(8,128)(2,1)S(1)}, bf16[128,128]{1,0:T(8,128)(2,1)}, u32[]{:S(2)}) copy-start(bf16[128,128]{1,0:T(8,128)(2,1)} %param.30) | copy-start | bytes 98308
  142.9 81.5 %copy-start.7 = (bf16[128,64]{0,1:T(8,128)(2,1)S(1)}, bf16[128,64]{0,1:T(8,128)(2,1)}, u32[]{:S(2)}) copy-start(bf16[128,64]{0,1:T(8,128)(2,1)} %param.31) | copy-start | bytes 49156
  142.9 81.5 %copy-start.12 = (f32[128]{0:T(128)S(1)}, f32[128]{0:T(128)}, u32[]{:S(2)}) copy-start(f32[128]{0:T(128)} %param.28) | copy-start | bytes 1540
  224.5 6.5 %copy-start.8 = (bf16[64,64]{1,0:T(8,128)(2,1)S(1)}, bf16[64,64]{1,0:T(8,128)(2,1)}, u32[]{:S(2)}) copy-start(bf16[64,64]{1,0:T(8,128)(2,1)} %param.32) | copy-start | bytes 24580
  224.5 6.5 %copy-start.13 = (bf16[64]{0:T(256)(128)(2,1)S(1)}, bf16[64]{0:T(256)(128)(2,1)}, u32[]{:S(2)}) copy-start(bf16[64]{0:T(256)(128)(2,1)} %param.33) | copy-start | bytes 388
  231.0 2.7 copy-start.4
  233.7 2.5 copy-start.1
Sparse Core Ops, SparseCore 0:
  48.8 172.5 all-gather.5
  239.2 104.8 all-gather.7
